TPU v7x, 32 devices: a whole 2x2x4 slice. The times are simulated.
32 devices in a mesh: modes: 4 (over y, core), gz: 8 (over z, x).
Axes of the slice: x: 2, y: 2, z: 4, core: 2. Of those that a mesh axis runs over, the one named last changes fastest.
Arguments:
- source_field: float32 [128, 2, 8, 2048], P('gz', None, None, 'modes'), may hold values from -0.075 to 0.075
- coupling_below: float32 [128], P('gz'), may hold values from 0.5 to 2
- coupling_above: float32 [128], P('gz'), may hold values from 0.5 to 2
- eigen_stream: float32 [8], replicated, may hold values from 0.000390625 to 0.015625
- eigen_span: float32 [2048], replicated, may hold values from 0.000390625 to 0.015625
Outputs:
- pressure: float32 [128, 2, 8, 2048], P('gz', None, 'modes')
All inputs are finite; a program needn't handle non-finite values.
Results may differ from a plain program's by a relative error of at most 0.0003.
Values sent between devices are 32-bit elements; how exact they have to be, the bound alone decides.
No kernel may reach another device: no remote copies, remote signals or barrier semaphores. Data moves between devices by JAX's collectives and lax.ppermute only.
A program may use at most 64 MiB of HBM per device.

v0:
```python
import jax
import jax.numpy as jnp
from jax import lax
from jax.sharding import PartitionSpec as P


def shifted(array, axis, by):
    count = lax.axis_size(axis)
    pairs = [(i, i + by) for i in range(count) if 0 <= i + by < count]
    return lax.ppermute(array, axis, pairs)


def thomas(lower_row, upper_row, spectral, sources, initial):
    row_count = sources.shape[0]

    def thomas_forward(carried, inputs):
        factor, partial_value = carried
        lower_val, upper_val, source_row = inputs
        pivots = lower_val + upper_val + spectral - lower_val * factor
        partial_value = (source_row + lower_val * partial_value) / pivots
        factor = upper_val / pivots
        return ((factor, partial_value), (factor, partial_value))

    _, (factors, partials) = lax.scan(
        thomas_forward,
        (jnp.zeros_like(spectral), initial),
        (lower_row, upper_row, sources),
        unroll=True,
    )
    retain = (jnp.arange(row_count) < row_count - 1).astype(jnp.float32)
    factors = factors * retain.reshape((row_count,) + (1,) * spectral.ndim)

    def thomas_backward(behind, inputs):
        factor, partial_value = inputs
        result = partial_value + factor * behind
        return (result, result)

    _, solved = lax.scan(
        thomas_backward, jnp.zeros_like(initial), (factors, partials), reverse=True, unroll=True
    )
    return solved


def reduced_solve(coeffs, right_side):

    def reduced_forward(carried, inputs):
        factor, partial_value = carried
        coeff_row, right_row = inputs
        pivots = coeff_row[1] - coeff_row[0] * factor
        factor = coeff_row[2] / pivots
        partial_value = (right_row - coeff_row[0] * partial_value) / pivots
        return ((factor, partial_value), (factor, partial_value))

    initial = (jnp.zeros_like(coeffs[0, 0]), jnp.zeros_like(right_side[0]))
    _, (factors, partials) = lax.scan(reduced_forward, initial, (coeffs, right_side), unroll=True)

    def reduced_backward(behind, inputs):
        factor, partial_value = inputs
        result = partial_value - factor * behind
        return (result, result)

    _, values = lax.scan(
        reduced_backward,
        jnp.zeros_like(right_side[0]),
        (factors, partials),
        reverse=True,
        unroll=True,
    )
    return values


def interfaces(planes, lower_row, upper_row, spectral):
    row_count = planes.shape[0]
    interior = row_count - 1
    modes_flat = planes.shape[2]
    last_mask = (jnp.arange(interior) == interior - 1).astype(jnp.float32) * upper_row[:interior]
    extra_source = last_mask[:, None, None] * jnp.ones((1, 1, modes_flat), jnp.float32)
    sources = jnp.concatenate(
        [planes[:interior], jnp.zeros((interior, 1, modes_flat), jnp.float32), extra_source], axis=1
    )
    initial = jnp.zeros((4, modes_flat), jnp.float32).at[2].set(1.0)
    solved = thomas(lower_row[:interior], upper_row[:interior], spectral, sources, initial)
    from_above = shifted(solved[0], "gz", -1)
    last_row = solved[interior - 1]
    lower_last = lower_row[row_count - 1]
    upper_last = upper_row[row_count - 1]
    coupling_down = -lower_last * last_row[2]
    central = (
        lower_last + upper_last + spectral - lower_last * last_row[3] - upper_last * from_above[2]
    )
    coupling_up = -upper_last * from_above[3]
    right_side = planes[row_count - 1] + lower_last * last_row[:2] + upper_last * from_above[:2]
    coeffs = jnp.stack([coupling_down, central, coupling_up])
    return (solved, coeffs, right_side)


def assemble(solved, interface_values):
    own_value = interface_values[:2]
    prev_value = interface_values[2:]
    inner = solved[:, :2] + solved[:, 2:3] * prev_value[None] + solved[:, 3:4] * own_value[None]
    return jnp.concatenate([inner, own_value[None]], axis=0)


def per_device(source_field, coupling_below, coupling_above, eigen_stream, eigen_span):
    arrived = lax.all_to_all(source_field, "modes", split_axis=2, concat_axis=3, tiled=True)
    row_count, _, kx_count, ky_count = arrived.shape
    partitions = lax.axis_size("gz")
    gz_index = lax.axis_index("gz")
    offset = lax.axis_index("modes") * kx_count
    stream_part = lax.dynamic_slice_in_dim(eigen_stream, offset, kx_count)
    spectral = stream_part[:, None] + eigen_span[None, :]
    global_row = gz_index * row_count + jnp.arange(row_count)
    lower_row = jnp.where(global_row == 0, 0.0, coupling_below)
    upper_row = jnp.where(global_row == row_count * partitions - 1, 0.0, coupling_above)
    modes_flat = kx_count * ky_count
    planes = arrived.reshape(row_count, 2, modes_flat)
    solved, coeffs, right_side = interfaces(planes, lower_row, upper_row, spectral.reshape(-1))
    coeff_items = coeffs.reshape(1, 3, kx_count, ky_count)
    right_items = right_side.reshape(1, 2, kx_count, ky_count)
    values = reduced_solve(
        lax.all_to_all(coeff_items, "gz", split_axis=3, concat_axis=0, tiled=True),
        lax.all_to_all(right_items, "gz", split_axis=3, concat_axis=0, tiled=True),
    )
    below_values = jnp.concatenate([jnp.zeros_like(values[:1]), values[:-1]], axis=0)
    paired = jnp.concatenate([values, below_values], axis=1)
    interface_values = lax.all_to_all(paired, "gz", split_axis=0, concat_axis=3, tiled=True)
    pressure = assemble(solved, interface_values.reshape(4, modes_flat))
    return pressure.reshape(row_count, 2, kx_count, ky_count)


def solution(mesh):
    in_specs = (P("gz", None, None, "modes"), P("gz"), P("gz"), P(), P())
    out_specs = P("gz", None, "modes", None)
    return jax.shard_map(
        per_device, mesh=mesh, in_specs=in_specs, out_specs=out_specs, check_vma=False
    )
```

profile of v0, /device:TPU:0, one launch (start us, length us, event | category | flops | bytes accessed | tf_op | source)
XLA Modules:
  0.0 153.8 jit_solution(18007086466472637981)
XLA Ops:
  0.0 2.2 %copy.91 = f32[16,2,8,512]{3,0,1,2:T(8,128)} copy(f32[16,2,8,512]{3,2,1,0:T(8,128)} %param.7) | data formatting | bytes 1048576 | tf_op args[0]
  2.2 4.3 %all-to-all-start = ((f32[16,2,8,512]{3,0,1,2:T(8,128)}), f32[16,2,8,512]{3,0,1,2:T(8,128)S(1)}, u32[]{:S(2)}, u32[]{:S(2)}) async-start(f32[16,2,8,512]{3,0,1,2:T(8,128)} %copy.91), calls=%async_computation | async-start | bytes 1048576 | tf_op jit(solution)/shard_map/all_to_all | solution.py:105
  6.5 0.7 fusion.116
  7.9 0.7 fusion.117
  12.3 0.8 divide_bitcast_fusion
  31.2 17.7 %subtract_divide_fusion = (f32[1,4096]{1,0:T(1,128)S(1)}, f32[1,4096]{1,0:T(1,128)S(1)}, f32[1,4096]{1,0:T(1,128)S(1)}, f32[1,4096]{1,0:T(1,128)S(1)}, f32[1,409...) fusion(f32[1,4096]{1,0:T(1,128)S(1)} %bitcast.585, ...), kind=kLoop, calls=%fused_computation.174 | loop fusion | flops 172032 | bytes 475248 | tf_op jit(solution)/shard_map/eval_jaxpr/div | solution.py:21
  49.8 17.6 %multiply_subtract_fusion = (f32[4096]{0:T(1024)S(1)}, f32[4096]{0:T(1024)S(1)}, f32[4096]{0:T(1024)S(1)}, f32[4096]{0:T(1024)S(1)}, f32[4096]{0:T(1024)S(1)}, /...) fusion(f32[4096]{0:T(1024)S(1)} %bitcast.584, ...), kind=kLoop, calls=%fused_computation.160 | loop fusion | flops 172032 | bytes 475248 | tf_op jit(solution)/shard_map/eval_jaxpr/sub | solution.py:19
  67.9 0.5 slice.459
  69.1 9.6 %multiply_add_fusion = (f32[4,4096]{1,0:T(4,128)S(1)}, f32[4,4096]{1,0:T(4,128)S(1)}) fusion(f32[4096]{0:T(1024)S(1)} %bitcast.545, f32[4096]{0:T(1024)S(1)} %bitcast.554, f32[4096]{0:T(1024)S(1)} %bitcast.527, f32[4096]{0:T(1024)S(1)} %bitcast.556, f32[4096]{0:T(1024)S(1)} %bitcast.530, f32[4096]{0:T(1024)S(1)} %bitcast.558, f32[4096]{0:T(1024)S(1)} %bitcast.533, ...), kind=kLoop, calls=%fused_computation.56 | loop fusion | flops 1212416 | bytes 1671228 | tf_op jit(solution)/shard_map/eval_jaxpr/add | solution.py:35
  78.7 1.3 collective-permute-start
  80.0 10.3 %add_dynamic-update-slice_fusion = (f32[15,4,4096]{2,1,0:T(4,128)}, f32[1,4,4096]{2,1,0:T(4,128)S(1)}, f32[1,4,4096]{2,1,0:T(4,128)S(1)}, f32[1,4,4096]{2,1,0:T(...) fusion(f32[4096]{0:T(1024)S(1)} %bitcast.567, ...), kind=kLoop, calls=%fused_computation.57 | loop fusion | flops 1212415 | bytes 2457660
  90.3 0.6 constant_dynamic-update-slice_fusion.13
  90.9 0.6 constant_dynamic-update-slice_fusion.12
  91.5 0.6 constant_dynamic-update-slice_fusion.11
  92.2 0.6 constant_dynamic-update-slice_fusion.10
  92.8 0.6 constant_dynamic-update-slice_fusion.9
  93.4 0.6 constant_dynamic-update-slice_fusion.8
  94.1 0.6 constant_dynamic-update-slice_fusion.7
  94.7 0.6 constant_dynamic-update-slice_fusion.6
  95.3 0.7 constant_dynamic-update-slice_fusion.5
  96.0 0.6 constant_dynamic-update-slice_fusion.4
  96.6 0.6 constant_dynamic-update-slice_fusion.3
  97.3 0.6 constant_dynamic-update-slice_fusion.2
  97.9 1.2 constant_dynamic-update-slice_fusion.1
  99.1 1.4 fusion.53
  100.6 1.3 fusion.18
  102.0 1.1 copy.93
  103.1 3.5 %reshape.3546 = f32[8,1,1024]{2,1,0:T(1,128)} reshape(f32[2048,1,2,2]{3,2,1,0:T(2,128)S(1)} %bitcast.511) | data formatting | bytes 65536
  106.6 7.7 %all-to-all-start.1 = ((f32[8,1,1024]{2,1,0:T(1,128)}), f32[8,1,1024]{2,1,0:T(1,128)S(1)}, u32[]{:S(2)}, u32[]{:S(2)}) async-start(f32[8,1,1024]{2,1,0:T(1,128)} %reshape.3546), calls=%async_computation.1 | async-start | bytes 65536 | tf_op jit(solution)/shard_map/all_to_all | solution.py:122
  114.3 1.1 copy.95
  115.4 3.6 %reshape.3548 = f32[8,1,1536]{2,1,0:T(1,128)} reshape(f32[2048,1,2,3]{3,2,1,0:T(2,128)S(1)} %bitcast.512) | data formatting | bytes 98304
  119.0 1.9 %all-to-all-done.1 = f32[8,1,1024]{2,1,0:T(1,128)S(1)} async-done(((f32[8,1,1024]{2,1,0:T(1,128)}), f32[8,1,1024]{2,1,0:T(1,128)S(1)}, u32[]{:S(2)}, u32[]{:S(2)}) %all-to-all-start.1) | async-done | bytes 32800 | tf_op jit(solution)/shard_map/all_to_all | solution.py:122
  121.0 4.1 %all-to-all-start.2 = ((f32[8,1,1536]{2,1,0:T(1,128)}), f32[8,1,1536]{2,1,0:T(1,128)S(1)}, u32[]{:S(2)}, u32[]{:S(2)}) async-start(f32[8,1,1536]{2,1,0:T(1,128)} %reshape.3548), calls=%async_computation.2 | async-start | bytes 98304 | tf_op jit(solution)/shard_map/all_to_all | solution.py:121
  125.0 1.2 constant_dynamic-update-slice_fusion
  126.2 0.5 broadcast.5415
  126.7 0.7 reduce.15
  127.5 3.2 %reshape.3547 = f32[2048,1,2,2]{3,2,1,0:T(2,128)S(1)} reshape(f32[8,1024]{1,0:T(8,128)S(1)} %reduce.15) | data formatting | bytes 65536
  130.7 0.9 copy.94
  131.8 0.7 reduce.14
  132.6 3.1 %reshape.3549 = f32[2048,1,2,3]{3,2,1,0:T(2,128)S(1)} reshape(f32[8,1536]{1,0:T(8,128)S(1)} %reduce.14) | data formatting | bytes 98304
  135.7 0.8 copy.123
  137.0 0.6 fusion.1
  137.6 5.8 %all-to-all-start.3 = ((f32[8,4,2,256]{3,2,1,0:T(2,128)}), f32[8,4,2,256]{3,2,1,0:T(2,128)S(1)}, u32[]{:S(2)}, u32[]{:S(2)}) async-start(f32[8,4,2,256]{3,2,1,0:T(2,128)} %fusion.1), calls=%async_computation.3 | async-start | bytes 131072 | tf_op jit(solution)/shard_map/all_to_all | solution.py:126
  143.4 2.0 %fusion.112 = (f32[15,1,4096]{2,1,0:T(1,128)S(1)}, f32[15,1,4096]{2,1,0:T(1,128)S(1)}) fusion(f32[15,4,4096]{2,1,0:T(4,128)} %constant_dynamic-update-slice_fusion), kind=kLoop, calls=%fused_computation.270 | loop fusion | bytes 983040 | tf_op jit(solution)/shard_map/slice | solution.py:100
  145.8 4.5 %all-to-all-done.3 = f32[8,4,2,256]{3,2,1,0:T(2,128)S(1)} async-done(((f32[8,4,2,256]{3,2,1,0:T(2,128)}), f32[8,4,2,256]{3,2,1,0:T(2,128)S(1)}, u32[]{:S(2)}, u32[]{:S(2)}) %all-to-all-start.3) | async-done | bytes 65568 | tf_op jit(solution)/shard_map/all_to_all | solution.py:126
  150.5 1.6 %fusion = f32[15,2,4096]{2,1,0:T(2,128)S(1)} fusion(f32[15,4,4096]{2,1,0:T(4,128)} %constant_dynamic-update-slice_fusion, f32[2,4096]{1,0:T(2,128)S(1)} %mul.2749, f32[15,4096]{1,0:T(8,128)S(1)} %bitcast.519, f32[2,4096]{1,0:T(2,128)S(1)} %mul.2744, f32[15,4096]{1,0:T(8,128)S(1)} %bitcast.518), kind=kLoop, calls=%fused_computation.4 | loop fusion | flops 491520 | bytes 1540096 | tf_op jit(solution)/shard_map/add | solution.py:100
  152.0 0.6 concatenate.39
  152.6 1.1 pad_maximum_fusion.1
  (95 shorter events, 3.6 us)
Async XLA Ops:
  0.0 6.5 %copy-start.4 = (f32[16]{0:T(128)S(1)}, f32[16]{0:T(128)}, u32[]{:S(2)}) copy-start(f32[16]{0:T(128)} %param.9) | copy-start | bytes 196
  0.0 6.5 %copy-start.3 = (f32[16]{0:T(128)S(1)}, f32[16]{0:T(128)}, u32[]{:S(2)}) copy-start(f32[16]{0:T(128)} %param.8) | copy-start | bytes 196
  0.0 12.2 %copy-start.5 = (f32[8]{0:T(128)S(1)}, f32[8]{0:T(128)}, u32[]{:S(2)}) copy-start(f32[8]{0:T(128)} %param.10) | copy-start | bytes 100
  0.0 12.3 %copy-start.2 = (f32[2048]{0:T(1024)S(1)}, f32[2048]{0:T(1024)}, u32[]{:S(2)}) copy-start(f32[2048]{0:T(1024)} %param.11) | copy-start | bytes 24580
  2.2 65.2 %all-to-all-start = ((f32[16,2,8,512]{3,0,1,2:T(8,128)}), f32[16,2,8,512]{3,0,1,2:T(8,128)S(1)}, u32[]{:S(2)}, u32[]{:S(2)}) async-start(f32[16,2,8,512]{3,0,1,2:T(8,128)} %copy.91), calls=%async_computation | async-start | bytes 1048576 | tf_op jit(solution)/shard_map/all_to_all | solution.py:105
  67.8 1.3 copy-start.1
  68.4 11.6 %copy-start = (f32[1,4,4096]{2,1,0:T(4,128)S(1)}, f32[1,4,4096]{2,1,0:T(4,128)}, u32[]{:S(2)}) copy-start(f32[1,4,4096]{2,1,0:T(4,128)} %constant.75.clone.1) | copy-start | bytes 196612
  78.7 20.5 %collective-permute-start = (f32[4,4096]{1,0:T(4,128)S(1)}, f32[4,4096]{1,0:T(4,128)S(1)}, u32[]{:S(2)}, u32[]{:S(2)}) collective-permute-start(f32[4,4096]{1,0:T(4,128)S(1)} %get-tuple-element.64), channel_id=1, source_target_pairs={{1,0},{2,1},{3,2},{4,3},{5,4},{6,5},{7,6},{9,8},{10,9},{11,10},{12... | collective-permute-start | bytes 196616 | tf_op jit(solution)/shard_map/ppermute | solution.py:10
  106.6 14.4 %all-to-all-start.1 = ((f32[8,1,1024]{2,1,0:T(1,128)}), f32[8,1,1024]{2,1,0:T(1,128)S(1)}, u32[]{:S(2)}, u32[]{:S(2)}) async-start(f32[8,1,1024]{2,1,0:T(1,128)} %reshape.3546), calls=%async_computation.1 | async-start | bytes 65536 | tf_op jit(solution)/shard_map/all_to_all | solution.py:122
  121.0 10.9 %all-to-all-start.2 = ((f32[8,1,1536]{2,1,0:T(1,128)}), f32[8,1,1536]{2,1,0:T(1,128)S(1)}, u32[]{:S(2)}, u32[]{:S(2)}) async-start(f32[8,1,1536]{2,1,0:T(1,128)} %reshape.3548), calls=%async_computation.2 | async-start | bytes 98304 | tf_op jit(solution)/shard_map/all_to_all | solution.py:121
  137.6 12.7 %all-to-all-start.3 = ((f32[8,4,2,256]{3,2,1,0:T(2,128)}), f32[8,4,2,256]{3,2,1,0:T(2,128)S(1)}, u32[]{:S(2)}, u32[]{:S(2)}) async-start(f32[8,4,2,256]{3,2,1,0:T(2,128)} %fusion.1), calls=%async_computation.3 | async-start | bytes 131072 | tf_op jit(solution)/shard_map/all_to_all | solution.py:126
where the time goes:
time: 155 us; the launch traced here: 154 us
  other arithmetic  71 us (46%)
  local copies, waits for them, and re-layouts  30.6 us (20%)
  starting transfers between devices  23.1 us (15%)
  between operations  22.5 us (15%)
  waiting for transfers between devices  6.71 us (4%)
    unnamed x69, local copies, waits for them, and re-layouts  20.1 us
    div x1, other arithmetic, thomas_forward(): factor = upper_val / pivots  17.7 us
    sub x1, other arithmetic, thomas_forward(): pivots = lower_val + upper_val + spectral - lower_val * factor  17.6 us
    unnamed x12, other arithmetic  16.4 us
    add x1, other arithmetic, thomas_backward(): result = partial_value + factor * behind  9.6 us
    all_to_all x1, starting transfers between devices, per_device(): lax.all_to_all(right_items, 'gz', split_axis=3, concat_axis=0, tiled=True)  7.67 us
    all_to_all x1, starting transfers between devices, per_device(): lax.all_to_all(paired, 'gz', split_axis=0, concat_axis=3, tiled=True)  5.8 us
    all_to_all x1, waiting for transfers between devices, per_device(): lax.all_to_all(paired, 'gz', split_axis=0, concat_axis=3, tiled=True)  4.54 us
  transfers between devices with their start and end apart: 5, of which 3 were waited for; matrix products, arithmetic and copies ran while one was open for 47% of the time, Pallas kernels for 0%

commit v1 on v0

--- a/solution.py
+++ b/solution.py
@@ -117,9 +117,18 @@
     solved, coeffs, right_side = interfaces(planes, lower_row, upper_row, spectral.reshape(-1))
     coeff_items = coeffs.reshape(1, 3, kx_count, ky_count)
     right_items = right_side.reshape(1, 2, kx_count, ky_count)
+    pair_layers_all_for = lambda across, page: jnp.concatenate(
+        lax.all_to_all(
+            jnp.stack(jnp.split(page, lax.axis_size(across), 3), 0),
+            axis_name=across,
+            split_axis=0,
+            concat_axis=0,
+        ),
+        0,
+    )
     values = reduced_solve(
         lax.all_to_all(coeff_items, "gz", split_axis=3, concat_axis=0, tiled=True),
-        lax.all_to_all(right_items, "gz", split_axis=3, concat_axis=0, tiled=True),
+        pair_layers_all_for("gz", right_items),
     )
     below_values = jnp.concatenate([jnp.zeros_like(values[:1]), values[:-1]], axis=0)
     paired = jnp.concatenate([values, below_values], axis=1)

time: 155 us -> 144 us (0.929)
  local copies, waits for them, and re-layouts: 30.6 us -> 21.4 us
  other arithmetic: 71 us -> 63.8 us
  waiting for transfers between devices: 6.71 us -> 13.2 us
    unnamed x69 -> x74, local copies, waits for them, and re-layouts: 20.1 us -> 13.9 us
    all_to_all x1, waiting for transfers between devices: 0.21 us -> 6.2 us  [per_device(): lax.all_to_all(coeff_items, 'gz', split_axis=3, concat_axis=0, tiled=True)]
    unnamed x12, other arithmetic: 16.4 us -> 11.8 us
    all_to_all x1, starting transfers between devices: 7.67 us -> 3.52 us  [per_device(): lax.all_to_all(jnp.stack(jnp.split(page, lax.axis_size(across), 3), 0), a...]
    all_to_all x1, starting transfers between devices: 4.06 us -> 7.67 us  [per_device(): lax.all_to_all(coeff_items, 'gz', split_axis=3, concat_axis=0, tiled=True)]
  transfers between devices with their start and end apart: 5 -> 5, of which waited for: 3 -> 3; matrix products, arithmetic and copies ran while one was open for 47% -> 40% of each run, Pallas kernels for 0% -> 0%
where the time goes in v1:
time: 144 us; the launch traced here: 142 us
  other arithmetic  63.8 us (44%)
  between operations  22.4 us (16%)
  starting transfers between devices  21.6 us (15%)
  local copies, waits for them, and re-layouts  21.4 us (15%)
  waiting for transfers between devices  13.2 us (9%)
    div x1, other arithmetic, thomas_forward(): factor = upper_val / pivots  17.7 us
    sub x1, other arithmetic, thomas_forward(): pivots = lower_val + upper_val + spectral - lower_val * factor  17.5 us
    unnamed x74, local copies, waits for them, and re-layouts  13.9 us
    unnamed x12, other arithmetic  11.8 us
    add x1, other arithmetic, thomas_backward(): result = partial_value + factor * behind  9.76 us
    all_to_all x1, starting transfers between devices, per_device(): lax.all_to_all(coeff_items, 'gz', split_axis=3, concat_axis=0, tiled=True)  7.67 us
    all_to_all x1, waiting for transfers between devices, per_device(): lax.all_to_all(coeff_items, 'gz', split_axis=3, concat_axis=0, tiled=True)  6.2 us
    all_to_all x1, waiting for transfers between devices, per_device(): lax.all_to_all(paired, 'gz', split_axis=0, concat_axis=3, tiled=True)  6.05 us
  transfers between devices with their start and end apart: 5, of which 3 were waited for; matrix products, arithmetic and copies ran while one was open for 40% of the time, Pallas kernels for 0%

profile of v1, /device:TPU:0, one launch (start us, length us, event | category | flops | bytes accessed | tf_op | source)
XLA Modules:
  0.0 142.3 jit_solution(15520847569386116250)
XLA Ops:
  0.0 2.2 %copy.88 = f32[16,2,8,512]{3,0,1,2:T(8,128)} copy(f32[16,2,8,512]{3,2,1,0:T(8,128)} %param.7) | data formatting | bytes 1048576 | tf_op args[0]
  2.2 4.3 %all-to-all-start = ((f32[16,2,8,512]{3,0,1,2:T(8,128)}), f32[16,2,8,512]{3,0,1,2:T(8,128)S(1)}, u32[]{:S(2)}, u32[]{:S(2)}) async-start(f32[16,2,8,512]{3,0,1,2:T(8,128)} %copy.88), calls=%async_computation | async-start | bytes 1048576 | tf_op jit(solution)/shard_map/all_to_all | solution.py:105
  6.5 0.7 fusion.116
  7.8 0.7 fusion.117
  12.2 0.7 divide_bitcast_fusion
  30.4 0.3 fusion.49
  31.1 17.7 %subtract_divide_fusion = (f32[1,4096]{1,0:T(1,128)S(1)}, f32[1,4096]{1,0:T(1,128)S(1)}, f32[1,4096]{1,0:T(1,128)S(1)}, f32[1,4096]{1,0:T(1,128)S(1)}, f32[1,409...) fusion(f32[1,4096]{1,0:T(1,128)S(1)} %bitcast.608, ...), kind=kLoop, calls=%fused_computation.182 | loop fusion | flops 172032 | bytes 475248 | tf_op jit(solution)/shard_map/eval_jaxpr/div | solution.py:21
  48.9 0.4 concatenate.33
  49.3 0.2 slice_multiply_fusion.6
  49.8 17.5 %multiply_subtract_fusion = (f32[4096]{0:T(1024)S(1)}, f32[4096]{0:T(1024)S(1)}, f32[4096]{0:T(1024)S(1)}, f32[4096]{0:T(1024)S(1)}, f32[4096]{0:T(1024)S(1)}, /...) fusion(f32[4096]{0:T(1024)S(1)} %bitcast.607, ...), kind=kLoop, calls=%fused_computation.168 | loop fusion | flops 172032 | bytes 475248 | tf_op jit(solution)/shard_map/eval_jaxpr/sub | solution.py:19
  67.3 0.3 copy.277
  67.7 0.5 slice.459
  68.3 0.2 mul.2487
  68.5 0.5 pad_maximum_fusion
  69.0 9.8 %multiply_add_fusion = (f32[4,4096]{1,0:T(4,128)S(1)}, f32[4,4096]{1,0:T(4,128)S(1)}) fusion(f32[4096]{0:T(1024)S(1)} %bitcast.571, f32[4096]{0:T(1024)S(1)} %bitcast.577, f32[4096]{0:T(1024)S(1)} %bitcast.553, f32[4096]{0:T(1024)S(1)} %bitcast.579, f32[4096]{0:T(1024)S(1)} %bitcast.556, f32[4096]{0:T(1024)S(1)} %bitcast.581, f32[4096]{0:T(1024)S(1)} %bitcast.559, ...), kind=kLoop, calls=%fused_computation.94 | loop fusion | flops 1212416 | bytes 1671228 | tf_op jit(solution)/shard_map/eval_jaxpr/add | solution.py:35
  78.7 1.3 collective-permute-start
  80.0 9.8 %constant_dynamic-update-slice_fusion.14 = (f32[15,4,4096]{2,1,0:T(4,128)S(1)}, f32[1,4,4096]{2,1,0:T(4,128)S(1)}, f32[1,4,4096]{2,1,0:T(4,128)S(1)}, f32[1,4,40...) fusion(f32[4096]{0:T(1024)S(1)} %bitcast.590, ...), kind=kLoop, calls=%fused_computation.39 | loop fusion | flops 1212415 | bytes 2457660
  90.2 0.7 constant_dynamic-update-slice_fusion.1
  90.9 0.7 constant_dynamic-update-slice_fusion
  91.6 1.2 fusion.18
  92.8 1.3 fusion.53
  94.2 0.6 constant_dynamic-update-slice_fusion.22
  94.8 0.6 constant_dynamic-update-slice_fusion.21
  95.4 0.6 constant_dynamic-update-slice_fusion.20
  96.0 0.6 constant_dynamic-update-slice_fusion.19
  96.6 0.6 constant_dynamic-update-slice_fusion.18
  97.2 0.6 constant_dynamic-update-slice_fusion.17
  97.7 0.6 constant_dynamic-update-slice_fusion.16
  98.4 1.1 copy.90
  99.5 3.6 %reshape.3547 = f32[8,1,1536]{2,1,0:T(1,128)} reshape(f32[2048,1,2,3]{3,2,1,0:T(2,128)S(1)} %bitcast.539) | data formatting | bytes 98304
  103.1 7.7 %all-to-all-start.2 = ((f32[8,1,1536]{2,1,0:T(1,128)}), f32[8,1,1536]{2,1,0:T(1,128)S(1)}, u32[]{:S(2)}, u32[]{:S(2)}) async-start(f32[8,1,1536]{2,1,0:T(1,128)} %reshape.3547), calls=%async_computation.2 | async-start | bytes 98304 | tf_op jit(solution)/shard_map/all_to_all | solution.py:130
  110.7 0.6 constant_dynamic-update-slice_fusion.15
  111.3 6.2 %all-to-all-done.2 = f32[8,1,1536]{2,1,0:T(1,128)S(1)} async-done(((f32[8,1,1536]{2,1,0:T(1,128)}), f32[8,1,1536]{2,1,0:T(1,128)S(1)}, u32[]{:S(2)}, u32[]{:S(2)}) %all-to-all-start.2) | async-done | bytes 49184 | tf_op jit(solution)/shard_map/all_to_all | solution.py:130
  117.5 3.5 %all-to-all-start.1 = ((f32[8,1,2,2,256]{4,3,2,1,0:T(2,128)}), f32[8,1,2,2,256]{4,3,2,1,0:T(2,128)S(1)}, u32[]{:S(2)}, u32[]{:S(2)}) async-start(f32[8,1,2,2,256]{4,3,2,1,0:T(2,128)} %constant_dynamic-update-slice_fusion.15), calls=%async_computation.1 | async-start | bytes 65536 | tf_op jit(solution)/shard_map/all_to_all | solution.py:121
  121.1 0.5 broadcast.5415
  121.6 0.8 reduce.14
  122.3 3.1 %reshape.3548 = f32[2048,1,2,3]{3,2,1,0:T(2,128)S(1)} reshape(f32[8,1536]{1,0:T(8,128)S(1)} %reduce.14) | data formatting | bytes 98304
  125.5 0.8 copy.118
  126.6 1.0 all-to-all-done.1
  127.7 0.6 fusion.1
  128.4 4.8 %all-to-all-start.3 = ((f32[8,4,2,256]{3,2,1,0:T(2,128)}), f32[8,4,2,256]{3,2,1,0:T(2,128)S(1)}, u32[]{:S(2)}, u32[]{:S(2)}) async-start(f32[8,4,2,256]{3,2,1,0:T(2,128)} %fusion.1), calls=%async_computation.3 | async-start | bytes 131072 | tf_op jit(solution)/shard_map/all_to_all | solution.py:135
  133.2 0.5 fusion.112
  133.7 0.1 copy.279
  133.9 0.1 copy.278
  134.0 6.1 %all-to-all-done.3 = f32[8,4,2,256]{3,2,1,0:T(2,128)S(1)} async-done(((f32[8,4,2,256]{3,2,1,0:T(2,128)}), f32[8,4,2,256]{3,2,1,0:T(2,128)S(1)}, u32[]{:S(2)}, u32[]{:S(2)}) %all-to-all-start.3) | async-done | bytes 65568 | tf_op jit(solution)/shard_map/all_to_all | solution.py:135
  140.2 0.4 fusion
  140.6 0.6 concatenate.39
  141.2 1.1 pad_maximum_fusion.1
  (98 shorter events, 1.5 us)
Async XLA Ops:
  0.0 6.5 %copy-start.4 = (f32[16]{0:T(128)S(1)}, f32[16]{0:T(128)}, u32[]{:S(2)}) copy-start(f32[16]{0:T(128)} %param.9) | copy-start | bytes 196
  0.0 6.5 %copy-start.3 = (f32[16]{0:T(128)S(1)}, f32[16]{0:T(128)}, u32[]{:S(2)}) copy-start(f32[16]{0:T(128)} %param.8) | copy-start | bytes 196
  0.0 12.1 %copy-start.5 = (f32[8]{0:T(128)S(1)}, f32[8]{0:T(128)}, u32[]{:S(2)}) copy-start(f32[8]{0:T(128)} %param.10) | copy-start | bytes 100
  0.0 12.2 %copy-start.2 = (f32[2048]{0:T(1024)S(1)}, f32[2048]{0:T(1024)}, u32[]{:S(2)}) copy-start(f32[2048]{0:T(1024)} %param.11) | copy-start | bytes 24580
  2.2 65.1 %all-to-all-start = ((f32[16,2,8,512]{3,0,1,2:T(8,128)}), f32[16,2,8,512]{3,0,1,2:T(8,128)S(1)}, u32[]{:S(2)}, u32[]{:S(2)}) async-start(f32[16,2,8,512]{3,0,1,2:T(8,128)} %copy.88), calls=%async_computation | async-start | bytes 1048576 | tf_op jit(solution)/shard_map/all_to_all | solution.py:105
  67.7 1.3 copy-start.1
  68.3 11.8 %copy-start = (f32[1,4,4096]{2,1,0:T(4,128)S(1)}, f32[1,4,4096]{2,1,0:T(4,128)}, u32[]{:S(2)}) copy-start(f32[1,4,4096]{2,1,0:T(4,128)} %constant.75.clone.1) | copy-start | bytes 196612
  78.7 12.9 %collective-permute-start = (f32[4,4096]{1,0:T(4,128)S(1)}, f32[4,4096]{1,0:T(4,128)S(1)}, u32[]{:S(2)}, u32[]{:S(2)}) collective-permute-start(f32[4,4096]{1,0:T(4,128)S(1)} %get-tuple-element.64), channel_id=1, source_target_pairs={{1,0},{2,1},{3,2},{4,3},{5,4},{6,5},{7,6},{9,8},{10,9},{11,10},{12... | collective-permute-start | bytes 196616 | tf_op jit(solution)/shard_map/ppermute | solution.py:10
  103.1 14.5 %all-to-all-start.2 = ((f32[8,1,1536]{2,1,0:T(1,128)}), f32[8,1,1536]{2,1,0:T(1,128)S(1)}, u32[]{:S(2)}, u32[]{:S(2)}) async-start(f32[8,1,1536]{2,1,0:T(1,128)} %reshape.3547), calls=%async_computation.2 | async-start | bytes 98304 | tf_op jit(solution)/shard_map/all_to_all | solution.py:130
  117.5 10.0 %all-to-all-start.1 = ((f32[8,1,2,2,256]{4,3,2,1,0:T(2,128)}), f32[8,1,2,2,256]{4,3,2,1,0:T(2,128)S(1)}, u32[]{:S(2)}, u32[]{:S(2)}) async-start(f32[8,1,2,2,256]{4,3,2,1,0:T(2,128)} %constant_dynamic-update-slice_fusion.15), calls=%async_computation.1 | async-start | bytes 65536 | tf_op jit(solution)/shard_map/all_to_all | solution.py:121
  128.4 11.7 %all-to-all-start.3 = ((f32[8,4,2,256]{3,2,1,0:T(2,128)}), f32[8,4,2,256]{3,2,1,0:T(2,128)S(1)}, u32[]{:S(2)}, u32[]{:S(2)}) async-start(f32[8,4,2,256]{3,2,1,0:T(2,128)} %fusion.1), calls=%async_computation.3 | async-start | bytes 131072 | tf_op jit(solution)/shard_map/all_to_all | solution.py:135
